TPU v7x, 256 devices: a whole 4x4x8 slice. The times are simulated.
256 devices in a mesh: lat: 16 (over x_lo, y, core), lon: 16 (over z, x_hi).
Axes of the slice: x: 4 (x_hi: 2, x_lo: 2; x = x_hi * 2 + x_lo), y: 4, z: 8, core: 2. Of those that a mesh axis runs over, the one named last changes fastest.
Arguments:
- current_sample: float32 [4, 512, 4096], P(None, 'lat', 'lon'), may hold values from -6 to 6
- churn_noise: float32 [4, 512, 4096], P(None, 'lat', 'lon'), may hold values from -6 to 6
- coarse_fields: float32 [12, 64, 512], P(None, 'lat', 'lon'), may hold values from -6 to 6
- tile_owner: int32 [16], replicated, may hold values from 0 to 15, each once
- input_kernel: bfloat16 [3, 3, 16, 128], replicated, may hold values from -0.5 to 0.5
- fine_first: bfloat16 [3, 3, 128, 128], replicated, may hold values from -0.1875 to 0.1875
- fine_second: bfloat16 [3, 3, 128, 128], replicated, may hold values from -0.1875 to 0.1875
- coarse_first: bfloat16 [3, 3, 128, 128], replicated, may hold values from -0.1875 to 0.1875
- coarse_second: bfloat16 [3, 3, 128, 128], replicated, may hold values from -0.1875 to 0.1875
- output_kernel: bfloat16 [3, 3, 128, 4], replicated, may hold values from -0.5 to 0.5
Outputs:
- next_sample: float32 [4, 512, 4096], P(None, 'lat', 'lon')
Inputs may be any that keep to these rules, and one draw needn't show every extreme that they name: `tile_owner`: each value is the row block's position along the bands; every stored block covers exactly one band.
All inputs are finite; a program needn't handle non-finite values.
Results may differ from a plain program's by a relative error of at most 0.0055.
Values may be sent and summed in bfloat16 or wider, within the bound.
No kernel may reach another device: no remote copies, remote signals or barrier semaphores. Data moves between devices by JAX's collectives and lax.ppermute only.
A program may use at most 64 MiB of HBM per device.

v0:
```python
import math

import jax
import jax.numpy as jnp
from jax import lax
from jax.experimental import pallas as pl
from jax.experimental.pallas import tpu as pltpu
from jax.sharding import PartitionSpec as P


RATIO = 8
CH = 128
ROWS = 32
COLS = 256
ROW_HALO = 9
COL_HALO = 16
EXT_ROWS = ROWS + 2 * ROW_HALO
EXT_COLS = COLS + 2 * COL_HALO
COARSE_COLS = EXT_COLS // RATIO
LANES = 384
SEGS = 16
LEN = EXT_COLS // SEGS
CLEN = LEN // 2
GROUPS = 8
NF, NF2, NC = 4, 4, 5
N1, N2, N3 = 24 // NF, 22 // NF2, 10 // NC

sigma_now = 1.0
sigma_hat = 1.2
sigma_next = 0.4
sigma_data = 0.5
CHURN = math.sqrt(sigma_hat**2 - sigma_now**2)
DENOM = sigma_hat**2 + sigma_data**2
HALF = math.sqrt(0.5)
BF = jnp.bfloat16
F32 = jnp.float32


def silu(v):
    h = 0.5 * v
    return h + h * jnp.tanh(h)


def put_row(dst, row, val, n):
    dst[row, 1 : n + 1] = val.astype(BF)
    dst[row, 0] = pltpu.roll(val[n - 1], 1, 0).astype(BF)
    dst[row, n + 1] = pltpu.roll(val[0], SEGS - 1, 0).astype(BF)


def pair_rows(r, rows, top, bottom):
    mirrored = jnp.logical_or(
        jnp.logical_and(top == 1, r < 0), jnp.logical_and(bottom == 1, r >= rows)
    )
    return jnp.where(mirrored, r + 2, r - 1), jnp.where(mirrored, -1, 1)


def conv_pairs(src, firsts, w, n):
    lhs = jnp.concatenate(
        [
            jnp.concatenate(
                [
                    src[base + step * k, b : b + n].reshape(n * SEGS, CH)
                    for k in range(4)
                    for b in range(3)
                ],
                axis=1,
            )
            for base, step in firsts
        ],
        axis=0,
    )
    zero = jnp.zeros((3 * CH, CH), BF)
    rhs = jnp.concatenate(
        [jnp.concatenate([w[...], zero], 0), jnp.concatenate([zero, w[...]], 0)], 1
    )
    acc = jnp.dot(lhs, rhs, preferred_element_type=F32).reshape(len(firsts), n, SEGS, 2 * CH)
    return [(acc[i, :, :, :CH], acc[i, :, :, CH:]) for i in range(len(firsts))]


def net_kernel(
    flags,
    x,
    cur,
    noise,
    w_in,
    w_f1,
    w_f2,
    w_c1,
    w_c2,
    w_out,
    out,
    a0,
    stem,
    act,
    hid,
    fine,
    pooled,
    cact,
    chid,
    merged,
    flat,
):
    top = flags[0]
    bottom = flags[1]

    i = lax.broadcasted_iota(jnp.int32, ((LEN + 2) * SEGS, LANES), 0)
    lane = lax.broadcasted_iota(jnp.int32, ((LEN + 2) * SEGS, LANES), 1)
    col = LEN * (i & (SEGS - 1)) + (i >> 4) - 1
    inside = jnp.logical_and(col >= 0, col < EXT_COLS)
    hit = jnp.logical_or(lane == col, lane == EXT_COLS + (col >> 3))
    place = jnp.where(jnp.logical_and(inside, hit), 1.0, 0.0).astype(BF)
    for g in range(GROUPS):
        part = x[96 * g : 96 * g + 128, :]
        val = lax.dot_general(place, part, (((1,), (1,)), ((), ())), preferred_element_type=F32)
        a0[g] = val.reshape(LEN + 2, SEGS, CH).astype(BF)

    act[0] = jnp.zeros((LEN + 2, SEGS, CH), BF)
    act[EXT_ROWS - 1] = jnp.zeros((LEN + 2, SEGS, CH), BF)
    chid[0] = jnp.zeros((CLEN + 2, SEGS, CH), BF)
    chid[21] = jnp.zeros((CLEN + 2, SEGS, CH), BF)

    def stem_body(g, carry):
        lhs = jnp.concatenate(
            [a0[g, b : b + LEN].reshape(LEN * SEGS, CH) for b in range(3)], axis=1
        )
        for j in range(3):
            r = 6 * g + 2 * j - 8
            _, step = pair_rows(r, ROWS, top, bottom)
            flip = jnp.where(step < 0, 1, 0)
            acc = jnp.dot(lhs, w_in[flip * 3 + j], preferred_element_type=F32)
            for h in range(2):
                val = acc[:, h * CH : (h + 1) * CH].reshape(LEN, SEGS, CH).astype(BF)
                stem[r + 8 + h] = val
                put_row(act, r + 9 + h, silu(val.astype(F32)), LEN)
        return carry

    lax.fori_loop(0, GROUPS, stem_body, 0)

    def first_body(p, carry):
        firsts = [pair_rows(2 * NF * p + 2 * i - 8, ROWS, top, bottom) for i in range(NF)]
        outs = conv_pairs(act, [(base + 9, step) for base, step in firsts], w_f1, LEN)
        for (base, step), (o0, o1) in zip(firsts, outs):
            put_row(hid, base + step + 8, silu(o0), LEN)
            put_row(hid, base + 2 * step + 8, silu(o1), LEN)
        return carry

    lax.fori_loop(0, N1, first_body, 0)

    def second_pairs(first, count):
        firsts = [pair_rows(2 * (first + i) - 6, ROWS, top, bottom) for i in range(count)]
        outs = conv_pairs(hid, [(base + 8, step) for base, step in firsts], w_f2, LEN)
        for i, ((base, step), (o0, o1)) in enumerate(zip(firsts, outs)):
            r0 = base + step
            r1 = base + 2 * step
            v0 = ((stem[r0 + 8].astype(F32) + o0) * HALF).astype(BF)
            v1 = ((stem[r1 + 8].astype(F32) + o1) * HALF).astype(BF)
            fine[r0 + 6] = v0
            fine[r1 + 6] = v1
            both = (v0.astype(F32) + v1.astype(F32)).reshape(CLEN, 2, SEGS, CH)
            mean = ((both[:, 0] + both[:, 1]) * 0.25).astype(BF)
            pooled[first + i] = mean
            put_row(cact, first + i, silu(mean.astype(F32)), CLEN)

    def second_body(p, carry):
        second_pairs(NF2 * p, NF2)
        return carry

    lax.fori_loop(0, N2, second_body, 0)
    second_pairs(NF2 * N2, 22 - NF2 * N2)

    def third_body(p, carry):
        firsts = [pair_rows(2 * NC * p + 2 * i - 2, ROWS // 2, top, bottom) for i in range(NC)]
        outs = conv_pairs(cact, [(base + 3, step) for base, step in firsts], w_c1, CLEN)
        for (base, step), (o0, o1) in zip(firsts, outs):
            put_row(chid, base + step + 3, silu(o0), CLEN)
            put_row(chid, base + 2 * step + 3, silu(o1), CLEN)
        return carry

    lax.fori_loop(0, N3, third_body, 0)

    def fourth_body(p, carry):
        firsts = [pair_rows(2 * NC * p + 2 * i - 2, ROWS // 2, top, bottom) for i in range(NC)]
        results = conv_pairs(chid, [(base + 3, step) for base, step in firsts], w_c2, CLEN)
        for (base, step), outs in zip(firsts, results):
            for h in range(2):
                cr = base + (h + 1) * step
                co = ((pooled[cr + 3].astype(F32) + outs[h]) * HALF).astype(BF).astype(F32)
                wide = jnp.broadcast_to(co[:, None], (CLEN, 2, SEGS, CH)).reshape(LEN, SEGS, CH)
                for q in range(2):
                    val = silu((fine[2 * cr + q + 6].astype(F32) + wide) * HALF)
                    put_row(merged, 2 * cr + q + 4, val, LEN)
        return carry

    lax.fori_loop(0, N3, fourth_body, 0)

    group_lane = lax.broadcasted_iota(jnp.int32, (LEN, SEGS, CH), 2) // 32
    rhs = jnp.concatenate([w_out[:, k * CH : (k + 1) * CH] for k in range(10)], axis=0)
    total = jnp.zeros((LEN, SEGS, CH), F32)
    for g in range(4):
        lhs = jnp.concatenate(
            [
                merged[8 * g + 3 + k].reshape((LEN + 2) * SEGS, CH)
                for k in range(10)
            ],
            axis=1,
        )
        z = jnp.dot(lhs, rhs, preferred_element_type=F32).reshape(LEN + 2, SEGS, CH)
        shift = 32 * g
        val = pltpu.roll(z[:LEN], shift, 2) if shift else z[:LEN]
        val = val + pltpu.roll(z[1 : LEN + 1], (96 + shift) % CH, 2)
        val = val + pltpu.roll(z[2:], (64 + shift) % CH, 2)
        total = jnp.where(group_lane == g, val, total)
    for l in range(LEN):
        flat[pl.ds(l, SEGS, stride=LEN), :] = total[l]
    rows = flat[COL_HALO : COL_HALO + COLS, :].T
    for g in range(4):
        for o in range(4):
            network = rows[32 * g + 8 * o : 32 * g + 8 * o + 8]
            at = pl.ds(8 * g, 8)
            perturbed = cur[o, at] + CHURN * noise[o, at]
            denoised = (
                sigma_data**2 / DENOM * perturbed
                + sigma_hat * sigma_data / math.sqrt(DENOM) * network
            )
            out[o, at] = perturbed + (sigma_next - sigma_hat) / sigma_hat * (perturbed - denoised)


def run_net(flags, x, cur, noise, w_in, w_f1, w_f2, w_c1, w_c2, w_out):
    vmem = pl.BlockSpec(memory_space=pltpu.VMEM)
    row = (LEN + 2, SEGS, CH)
    crow = (CLEN + 2, SEGS, CH)
    return pl.pallas_call(
        net_kernel,
        out_shape=jax.ShapeDtypeStruct((4, ROWS, COLS), F32),
        in_specs=[pl.BlockSpec(memory_space=pltpu.SMEM)] + [vmem] * 9,
        out_specs=vmem,
        scratch_shapes=[
            pltpu.VMEM((GROUPS,) + row, BF),
            pltpu.VMEM((48, LEN, SEGS, CH), BF),
            pltpu.VMEM((EXT_ROWS,) + row, BF),
            pltpu.VMEM((48,) + row, BF),
            pltpu.VMEM((44, LEN, SEGS, CH), BF),
            pltpu.VMEM((22, CLEN, SEGS, CH), BF),
            pltpu.VMEM((22,) + crow, BF),
            pltpu.VMEM((22,) + crow, BF),
            pltpu.VMEM((40,) + row, BF),
            pltpu.VMEM((EXT_COLS, CH), F32),
        ],
        compiler_params=pltpu.CompilerParams(vmem_limit_bytes=58 * 1024 * 1024),
        name="net",
    )(flags, x, cur, noise, w_in, w_f1, w_f2, w_c1, w_c2, w_out)


def stem_weights(kernel):
    tables = []
    for k in (kernel, kernel[::-1]):
        k = k.transpose(1, 0, 2, 3)
        for j in range(3):
            first = jnp.pad(k, ((0, 0), (2 * j, 5 - 2 * j), (0, 0), (0, 0)))
            second = jnp.pad(k, ((0, 0), (2 * j + 1, 4 - 2 * j), (0, 0), (0, 0)))
            tables.append(jnp.concatenate([first, second], axis=3).reshape(3 * 8 * 16, 2 * CH))
    return jnp.stack(tables)


def output_weights(kernel):
    per_row = []
    for r in range(8):
        per_row.append(jnp.pad(kernel, ((r, 7 - r), (0, 0), (0, 0), (0, 0))))
    w = jnp.stack(per_row)
    w = w.transpose(3, 1, 2, 4, 0).reshape(CH, 10, 96)
    return jnp.pad(w, ((0, 0), (0, 0), (0, 32))).reshape(CH, 10 * CH)


def swap(block, pairs):
    return lax.ppermute(block, ("lat", "lon"), pairs)


def device(lat, lon):
    return lat * 16 + lon % 16


def exchange(net_in, coarse, tile_owner, lat):
    is_top, is_bottom = lat == 0, lat == 15
    first = net_in[:, :ROW_HALO].reshape(72, CH)
    last = net_in[:, ROWS - ROW_HALO :].reshape(72, CH)
    stored = coarse.reshape(12, CH)
    dest = lax.broadcasted_iota(jnp.int32, (16, 1, 1), 0)
    rows = jnp.where(
        dest == lat + 1, last[None], jnp.where(dest == lat - 1, first[None], jnp.zeros_like(first[None]))
    )
    sent = jnp.concatenate([rows, jnp.broadcast_to(stored[None], (16, 12, CH))], axis=1)
    got = lax.all_to_all(sent, "lat", 0, 0, tiled=True)
    above = jnp.maximum(lat - 1, 0)
    below = jnp.minimum(lat + 1, 15)

    def rows_from(i):
        return lax.dynamic_slice_in_dim(got, i, 1, 0)[0, :72].reshape(4, ROW_HALO, COLS)

    def coarse_from(i):
        return lax.dynamic_slice_in_dim(got, tile_owner[i], 1, 0)[0, 72:].reshape(12, 4, 32)

    own = coarse_from(lat)
    edge = jnp.where(is_bottom, own[:, 2:].reshape(6, CH), own[:, :2].reshape(6, CH))
    across = swap(
        jnp.concatenate([jnp.where(is_bottom, last, first), edge], axis=0),
        [(device(i, q), device(i, q + 8)) for i in range(16) for q in range(16)],
    )
    pole = across[:72].reshape(4, ROW_HALO, COLS)[:, ::-1]
    cpole = across[72:].reshape(12, 2, 32)[:, ::-1]
    north = jnp.where(is_top, pole, rows_from(above))
    south = jnp.where(is_bottom, pole, rows_from(below))
    cnorth = jnp.where(is_top, cpole, coarse_from(above)[:, 2:])
    csouth = jnp.where(is_bottom, cpole, coarse_from(below)[:, :2])
    tall = jnp.concatenate([north, net_in, south], axis=1)
    ctall = jnp.concatenate([cnorth, own, csouth], axis=1)

    def pack(fine, crs):
        crs = jnp.pad(crs.reshape(192), (0, 64)).reshape(2, CH)
        return jnp.concatenate([fine.reshape(25, CH), crs], axis=0)

    def unpack(block):
        fine = block[:25].reshape(4, EXT_ROWS, COL_HALO)
        return fine, block[25:].reshape(256)[:192].reshape(12, 8, 2)

    east = pack(tall[:, :, COLS - COL_HALO :], ctall[:, :, 30:])
    west = pack(tall[:, :, :COL_HALO], ctall[:, :, :2])
    odd = lax.axis_index("lon") % 2 == 1
    near = swap(
        jnp.where(odd, west, east),
        [(device(i, q), device(i, q ^ 1)) for i in range(16) for q in range(16)],
    )
    far = swap(
        jnp.where(odd, east, west),
        [(device(i, q), device(i, q + 1 if q % 2 else q - 1)) for i in range(16) for q in range(16)],
    )
    left, cleft = unpack(jnp.where(odd, near, far))
    right, cright = unpack(jnp.where(odd, far, near))
    wide = jnp.concatenate([left, tall, right], axis=2)
    cwide = jnp.concatenate([cleft, ctall, cright], axis=2)
    wide = jnp.pad(wide, ((0, 0), (0, 0), (0, LANES - EXT_COLS))).transpose(1, 0, 2)
    cwide = jnp.pad(cwide, ((0, 0), (0, 0), (EXT_COLS, LANES - EXT_COLS - COARSE_COLS))).transpose(1, 0, 2)
    cwide = jnp.repeat(cwide, RATIO, axis=0)[RATIO - 1 : RATIO - 1 + EXT_ROWS]
    return jnp.concatenate([wide, cwide], axis=1).reshape(EXT_ROWS * 16, LANES)


def body(
    current_sample,
    churn_noise,
    coarse_fields,
    tile_owner,
    input_kernel,
    fine_first,
    fine_second,
    coarse_first,
    coarse_second,
    output_kernel,
):
    lat = lax.axis_index("lat")
    scale_in = 1.0 / math.sqrt(DENOM)
    net_in = ((current_sample + CHURN * churn_noise) * scale_in).astype(BF)
    x = exchange(net_in, coarse_fields.astype(BF), tile_owner, lat)
    flags = jnp.stack([(lat == 0).astype(jnp.int32), (lat == 15).astype(jnp.int32)])
    return run_net(
        flags,
        x,
        current_sample,
        churn_noise,
        stem_weights(input_kernel),
        fine_first.reshape(9 * CH, CH),
        fine_second.reshape(9 * CH, CH),
        coarse_first.reshape(9 * CH, CH),
        coarse_second.reshape(9 * CH, CH),
        output_weights(output_kernel),
    )


def solution(mesh):
    placed = (P(None, "lat", "lon"),) * 3 + (P(),) * 7
    return jax.shard_map(
        body, mesh=mesh, in_specs=placed, out_specs=P(None, "lat", "lon"), check_vma=False
    )
```

profile of v0, /device:TPU:128, one launch (start us, length us, event | category | flops | bytes accessed | tf_op | source)
XLA Modules:
  0.0 64.5 jit_solution(14921799002450014835)
XLA Ops:
  0.0 1.0 %multiply_convert_fusion = bf16[4,32,256]{2,1,0:T(8,128)(2,1)S(1)} fusion(f32[4,32,256]{2,1,0:T(8,128)} %cur.1, f32[4,32,256]{2,1,0:T(8,128)} %noise.1), kind=kLoop, calls=%fused_computation.37 | loop fusion | flops 131072 | bytes 327680 | tf_op jit(solution)/shard_map/convert_element_type | solution.py:360
  1.1 0.7 %convert_element_type.52 = bf16[12,4,32]{2,1,0:T(4,128)(2,1)S(1)} convert(f32[12,4,32]{2,1,0:T(4,128)} %param.12) | non-fusion elementwise | flops 1536 | bytes 9216 | tf_op jit(solution)/shard_map/convert_element_type | solution.py:361
  1.9 0.1 broadcast_in_dim.56
  2.0 0.1 select_select_fusion
  2.1 0.8 %pad_maximum_fusion.1 = bf16[16,84,128]{2,1,0:T(8,128)(2,1)} fusion(bf16[16,12,128]{2,1,0:T(8,128)(2,1)S(1)} %broadcast_in_dim.57, bf16[16,72,128]{2,1,0:T(8,128)(2,1)S(1)} %select_select_fusion), kind=kLoop, calls=%fused_computation.15 | loop fusion | flops 688128 | bytes 688128 | tf_op jit(solution)/shard_map/concatenate | solution.py:291
  2.9 5.5 %all-to-all-start = ((bf16[16,84,128]{2,1,0:T(8,128)(2,1)}), bf16[16,84,128]{2,1,0:T(8,128)(2,1)S(1)}, u32[]{:S(2)}, u32[]{:S(2)}) async-start(bf16[16,84,128]{2,1,0:T(8,128)(2,1)} %pad_maximum_fusion.1), calls=%async_computation | async-start | bytes 720896 | tf_op jit(solution)/shard_map/all_to_all | solution.py:292
  8.4 0.7 %fusion.38 = (s32[1]{0:T(128)}, s32[1]{0:T(128)}, s32[1]{0:T(128)}) fusion(s32[16]{0:T(128)S(1)} %copy-done.3, s32[]{:T(128)S(6)} %max.3, s32[]{:T(128)S(6)} %select_n.106, s32[]{:T(128)S(6)} %select_n.112), kind=kLoop, calls=%fused_computation.89 | loop fusion | bytes 36 | tf_op jit(solution)/shard_map/dynamic_slice | solution.py:300
  13.1 0.6 copy-done.1
  15.9 1.6 %all-to-all-done = bf16[16,84,128]{2,1,0:T(8,128)(2,1)S(1)} async-done(((bf16[16,84,128]{2,1,0:T(8,128)(2,1)}), bf16[16,84,128]{2,1,0:T(8,128)(2,1)S(1)}, u32[]{:S(2)}, u32[]{:S(2)}) %all-to-all-start) | async-done | bytes 344096 | tf_op jit(solution)/shard_map/all_to_all | solution.py:292
  17.5 0.1 reshape_squeeze.15
  17.7 0.1 collective-permute-start
  18.0 7.4 %collective-permute-done = bf16[78,128]{1,0:T(8,128)(2,1)S(1)} collective-permute-done((bf16[78,128]{1,0:T(8,128)(2,1)S(1)}, bf16[78,128]{1,0:T(8,128)(2,1)S(1)}, u32[]{:S(2)}, u32[]{:S(2)}) %collective-permute-start) | collective-permute-done | bytes 20000 | tf_op jit(solution)/shard_map/ppermute | solution.py:275
  25.5 0.1 rev.9
  25.7 0.1 fusion.35
  25.8 0.1 reshape.88
  25.9 0.1 reshape.92
  26.3 0.1 reshape.93
  26.4 0.1 reshape.90
  26.6 2.8 %collective-permute-start.1 = (bf16[27,128]{1,0:T(8,128)(2,1)S(1)}, bf16[27,128]{1,0:T(8,128)(2,1)S(1)}, u32[]{:S(2)}, u32[]{:S(2)}) collective-permute-start(bf16[27,128]{1,0:T(8,128)(2,1)S(1)} %get-tuple-element.24), channel_id=1, source_target_pairs={{0,1},{1,0},{2,3},{3,2},{4,5},{5,4},{6,7},{7,6},{8,9},{9,8},{10,11... | collective-permute-start | bytes 20744 | tf_op jit(solution)/shard_map/ppermute | solution.py:275
  29.4 0.3 collective-permute-start.2
  29.8 0.6 add_convert_fusion.flags
  30.5 0.9 %copy.37.w_out = bf16[128,1280]{1,0:T(8,128)(2,1)} copy(bf16[128,1280]{0,1:T(8,128)(2,1)S(1)} %bitcast.51) | data formatting | bytes 655360 | tf_op jit(solution)/shard_map/reshape | solution.py:271
  31.4 0.5 collective-permute-done.1
  31.8 4.8 %collective-permute-done.2 = bf16[27,128]{1,0:T(8,128)(2,1)S(1)} collective-permute-done((bf16[27,128]{1,0:T(8,128)(2,1)S(1)}, bf16[27,128]{1,0:T(8,128)(2,1)S(1)}, u32[]{:S(2)}, u32[]{:S(2)}) %collective-permute-start.2) | collective-permute-done | bytes 6944 | tf_op jit(solution)/shard_map/ppermute | solution.py:275
  36.7 0.1 reshape.95
  36.8 0.1 reshape.96
  36.9 0.2 fusion.25
  37.2 0.2 slice.98
  37.3 0.2 slice.101
  37.5 0.1 fusion.29
  37.8 1.1 %pad_maximum_fusion = bf16[50,16,384]{2,1,0:T(8,128)(2,1)} fusion(bf16[50,12,384]{2,1,0:T(8,128)(2,1)S(1)} %slice.122, bf16[50,4,384]{2,1,0:T(4,128)(2,1)S(1)} %copy.29), kind=kLoop, calls=%fused_computation | loop fusion | flops 1228800 | bytes 1228800 | tf_op jit(solution)/shard_map/concatenate | solution.py:343
  38.9 25.6 %net.1 = f32[4,32,256]{2,1,0:T(8,128)} custom-call(s32[2]{0:T(128)} %add_convert_fusion.flags, bf16[800,384]{1,0:T(8,128)(2,1)} %bitcast.50, f32[4,32,256]{2,1,0:T(8,128)} %cur.1, f32[4,32,256]{2,1,0:T(8,128)} %noise.1, bf16[6,384,256]{2,1,0:T(8,128)(2,1)} %copy-done, bf16[1152,128]{1,0:T(8,128)(2,1)} %bitcast.60, bf16[1152,128]{1,0:T(8,128)(2,1)} %bitcast.61, ...), custom_call_target="tpu_custom_call" | custom-call | tf_op jit(solution)/shard_map/net/pallas_call | solution.py:232
  (69 shorter events, 1.6 us)
Async XLA Ops:
  0.0 8.4 %copy-start.3 = (s32[16]{0:T(128)S(1)}, s32[16]{0:T(128)}, u32[]{:S(2)}) copy-start(s32[16]{0:T(128)} %param.13) | copy-start | bytes 196
  1.0 11.8 %copy-start.2 = (bf16[3,3,16,128]{3,2,1,0:T(8,128)(2,1)S(1)}, bf16[3,3,16,128]{3,2,1,0:T(8,128)(2,1)}, u32[]{:S(2)}) copy-start(bf16[3,3,16,128]{3,2,1,0:T(8,128)(2,1)} %param.14) | copy-start | bytes 110596
  2.9 14.6 %all-to-all-start = ((bf16[16,84,128]{2,1,0:T(8,128)(2,1)}), bf16[16,84,128]{2,1,0:T(8,128)(2,1)S(1)}, u32[]{:S(2)}, u32[]{:S(2)}) async-start(bf16[16,84,128]{2,1,0:T(8,128)(2,1)} %pad_maximum_fusion.1), calls=%async_computation | async-start | bytes 720896 | tf_op jit(solution)/shard_map/all_to_all | solution.py:292
  13.0 0.7 %copy-start.1 = (bf16[3,3,128,4]{2,3,1,0:T(4,128)(2,1)S(1)}, bf16[3,3,128,4]{2,3,1,0:T(4,128)(2,1)}, u32[]{:S(2)}) copy-start(bf16[3,3,128,4]{2,3,1,0:T(4,128)(2,1)} %param.19) | copy-start | bytes 27652
  15.8 14.6 %copy-start = (bf16[6,384,256]{2,1,0:T(8,128)(2,1)}, bf16[6,384,256]{2,1,0:T(8,128)(2,1)S(1)}, u32[]{:S(2)}) copy-start(bf16[6,384,256]{2,1,0:T(8,128)(2,1)S(1)} %constant_dynamic-update-slice_fusion.w_in) | copy-start | bytes 3538948
  17.7 7.8 %collective-permute-start = (bf16[78,128]{1,0:T(8,128)(2,1)S(1)}, bf16[78,128]{1,0:T(8,128)(2,1)S(1)}, u32[]{:S(2)}, u32[]{:S(2)}) collective-permute-start(bf16[78,128]{1,0:T(8,128)(2,1)S(1)} %pad_maximum_fusion.4), channel_id=1, source_target_pairs={{0,8},{1,9},{2,10},{3,11},{4,12},{5,13},{6,14},{7,15},{8,0},{9,1},... | collective-permute-start | bytes 59912 | tf_op jit(solution)/shard_map/ppermute | solution.py:275
  26.6 5.2 %collective-permute-start.1 = (bf16[27,128]{1,0:T(8,128)(2,1)S(1)}, bf16[27,128]{1,0:T(8,128)(2,1)S(1)}, u32[]{:S(2)}, u32[]{:S(2)}) collective-permute-start(bf16[27,128]{1,0:T(8,128)(2,1)S(1)} %get-tuple-element.24), channel_id=1, source_target_pairs={{0,1},{1,0},{2,3},{3,2},{4,5},{5,4},{6,7},{7,6},{8,9},{9,8},{10,11... | collective-permute-start | bytes 20744 | tf_op jit(solution)/shard_map/ppermute | solution.py:275
  29.4 7.3 %collective-permute-start.2 = (bf16[27,128]{1,0:T(8,128)(2,1)S(1)}, bf16[27,128]{1,0:T(8,128)(2,1)S(1)}, u32[]{:S(2)}, u32[]{:S(2)}) collective-permute-start(bf16[27,128]{1,0:T(8,128)(2,1)S(1)} %get-tuple-element.25), channel_id=1, source_target_pairs={{0,15},{1,2},{2,1},{3,4},{4,3},{5,6},{6,5},{7,8},{8,7},{9,10},{10,... | collective-permute-start | bytes 20744 | tf_op jit(solution)/shard_map/ppermute | solution.py:275
where the time goes:
time: 64.9 us; the launch traced here: 64.5 us
  Pallas kernels  25.6 us (39%)
  waiting for transfers between devices  14.3 us (22%)
  starting transfers between devices  8.75 us (13%)
  between operations  6.13 us (9%)
  other arithmetic  4.88 us (8%)
  local copies, waits for them, and re-layouts  4.84 us (7%)
    pallas_call x1, Pallas kernels, run_net(): pl.pallas_call(net_kernel, out_shape=jax.ShapeDtypeStruct((4, ROWS, COLS)...  25.6 us
    ppermute x3, waiting for transfers between devices, swap(): return lax.ppermute(block, ('lat', 'lon'), pairs)  12.7 us
    all_to_all x1, starting transfers between devices, exchange(): got = lax.all_to_all(sent, 'lat', 0, 0, tiled=True)  5.5 us
    ppermute x3, starting transfers between devices, swap(): return lax.ppermute(block, ('lat', 'lon'), pairs)  3.25 us
    all_to_all x1, waiting for transfers between devices, exchange(): got = lax.all_to_all(sent, 'lat', 0, 0, tiled=True)  1.57 us
  transfers between devices with their start and end apart: 4, of which 4 were waited for; matrix products, arithmetic and copies ran while one was open for 5% of the time, Pallas kernels for 0%

commit v1 on v0

--- a/solution.py
+++ b/solution.py
@@ -82,13 +82,20 @@
     x,
     cur,
     noise,
+    w_in_src,
+    w_f1_src,
+    w_f2_src,
+    w_c1_src,
+    w_c2_src,
+    w_out_src,
+    out,
     w_in,
     w_f1,
     w_f2,
     w_c1,
     w_c2,
     w_out,
-    out,
+    sems,
     a0,
     stem,
     act,
@@ -102,6 +109,21 @@
 ):
     top = flags[0]
     bottom = flags[1]
+    copies = [
+        pltpu.make_async_copy(src, dst, sems.at[n])
+        for n, (src, dst) in enumerate(
+            [
+                (w_in_src, w_in),
+                (w_f1_src, w_f1),
+                (w_f2_src, w_f2),
+                (w_c1_src, w_c1),
+                (w_c2_src, w_c2),
+                (w_out_src, w_out),
+            ]
+        )
+    ]
+    for copy in copies:
+        copy.start()
 
     i = lax.broadcasted_iota(jnp.int32, ((LEN + 2) * SEGS, LANES), 0)
     lane = lax.broadcasted_iota(jnp.int32, ((LEN + 2) * SEGS, LANES), 1)
@@ -119,22 +141,29 @@
     chid[0] = jnp.zeros((CLEN + 2, SEGS, CH), BF)
     chid[21] = jnp.zeros((CLEN + 2, SEGS, CH), BF)
 
-    def stem_body(g, carry):
+    def stem_groups(groups, j, w):
         lhs = jnp.concatenate(
-            [a0[g, b : b + LEN].reshape(LEN * SEGS, CH) for b in range(3)], axis=1
+            [
+                jnp.concatenate(
+                    [a0[g, b : b + LEN].reshape(LEN * SEGS, CH) for b in range(3)], axis=1
+                )
+                for g in groups
+            ],
+            axis=0,
         )
-        for j in range(3):
+        acc = jnp.dot(lhs, w, preferred_element_type=F32).reshape(len(groups), LEN, SEGS, 2 * CH)
+        for n, g in enumerate(groups):
             r = 6 * g + 2 * j - 8
-            _, step = pair_rows(r, ROWS, top, bottom)
-            flip = jnp.where(step < 0, 1, 0)
-            acc = jnp.dot(lhs, w_in[flip * 3 + j], preferred_element_type=F32)
             for h in range(2):
-                val = acc[:, h * CH : (h + 1) * CH].reshape(LEN, SEGS, CH).astype(BF)
+                val = acc[n, :, :, h * CH : (h + 1) * CH].astype(BF)
                 stem[r + 8 + h] = val
                 put_row(act, r + 9 + h, silu(val.astype(F32)), LEN)
-        return carry
-
-    lax.fori_loop(0, GROUPS, stem_body, 0)
+
+    copies[0].wait()
+    for j in range(3):
+        stem_groups([1, 2, 3, 4, 5, 6][j == 0 : 6 - (j == 2)], j, w_in[j])
+        stem_groups([0, 1] if j == 0 else [0], j, w_in[3 * top + j])
+        stem_groups([6, 7] if j == 2 else [7], j, w_in[3 * bottom + j])
 
     def first_body(p, carry):
         firsts = [pair_rows(2 * NF * p + 2 * i - 8, ROWS, top, bottom) for i in range(NF)]
@@ -144,6 +173,7 @@
             put_row(hid, base + 2 * step + 8, silu(o1), LEN)
         return carry
 
+    copies[1].wait()
     lax.fori_loop(0, N1, first_body, 0)
 
     def second_pairs(first, count):
@@ -165,6 +195,7 @@
         second_pairs(NF2 * p, NF2)
         return carry
 
+    copies[2].wait()
     lax.fori_loop(0, N2, second_body, 0)
     second_pairs(NF2 * N2, 22 - NF2 * N2)
 
@@ -176,6 +207,7 @@
             put_row(chid, base + 2 * step + 3, silu(o1), CLEN)
         return carry
 
+    copies[3].wait()
     lax.fori_loop(0, N3, third_body, 0)
 
     def fourth_body(p, carry):
@@ -191,8 +223,10 @@
                     put_row(merged, 2 * cr + q + 4, val, LEN)
         return carry
 
+    copies[4].wait()
     lax.fori_loop(0, N3, fourth_body, 0)
 
+    copies[5].wait()
     group_lane = lax.broadcasted_iota(jnp.int32, (LEN, SEGS, CH), 2) // 32
     rhs = jnp.concatenate([w_out[:, k * CH : (k + 1) * CH] for k in range(10)], axis=0)
     total = jnp.zeros((LEN, SEGS, CH), F32)
@@ -232,9 +266,18 @@
     return pl.pallas_call(
         net_kernel,
         out_shape=jax.ShapeDtypeStruct((4, ROWS, COLS), F32),
-        in_specs=[pl.BlockSpec(memory_space=pltpu.SMEM)] + [vmem] * 9,
+        in_specs=[pl.BlockSpec(memory_space=pltpu.SMEM)]
+        + [vmem] * 3
+        + [pl.BlockSpec(memory_space=pl.ANY)] * 6,
         out_specs=vmem,
         scratch_shapes=[
+            pltpu.VMEM((6, 3 * CH, 2 * CH), BF),
+            pltpu.VMEM((9 * CH, CH), BF),
+            pltpu.VMEM((9 * CH, CH), BF),
+            pltpu.VMEM((9 * CH, CH), BF),
+            pltpu.VMEM((9 * CH, CH), BF),
+            pltpu.VMEM((CH, 10 * CH), BF),
+            pltpu.SemaphoreType.DMA((6,)),
             pltpu.VMEM((GROUPS,) + row, BF),
             pltpu.VMEM((48, LEN, SEGS, CH), BF),
             pltpu.VMEM((EXT_ROWS,) + row, BF),

time: 64.9 us -> 63.5 us (0.978)
  Pallas kernels: 25.6 us -> 24 us
    pallas_call x1, Pallas kernels: 25.6 us -> 24 us  [run_net(): pl.pallas_call(net_kernel, out_shape=jax.ShapeDtypeStruct((4, ROWS, COLS)...]
where the time goes in v1:
time: 63.5 us; the launch traced here: 63 us
  Pallas kernels  24 us (38%)
  waiting for transfers between devices  14.3 us (23%)
  starting transfers between devices  8.75 us (14%)
  between operations  6.29 us (10%)
  other arithmetic  4.88 us (8%)
  local copies, waits for them, and re-layouts  4.84 us (8%)
    pallas_call x1, Pallas kernels, run_net(): pl.pallas_call(net_kernel, out_shape=jax.ShapeDtypeStruct((4, ROWS, COLS)...  24 us
    ppermute x3, waiting for transfers between devices, swap(): return lax.ppermute(block, ('lat', 'lon'), pairs)  12.7 us
    all_to_all x1, starting transfers between devices, exchange(): got = lax.all_to_all(sent, 'lat', 0, 0, tiled=True)  5.5 us
    ppermute x3, starting transfers between devices, swap(): return lax.ppermute(block, ('lat', 'lon'), pairs)  3.25 us
    all_to_all x1, waiting for transfers between devices, exchange(): got = lax.all_to_all(sent, 'lat', 0, 0, tiled=True)  1.57 us
  transfers between devices with their start and end apart: 4, of which 4 were waited for; matrix products, arithmetic and copies ran while one was open for 5% of the time, Pallas kernels for 0%

profile of v1, /device:TPU:128, one launch (start us, length us, event | category | flops | bytes accessed | tf_op | source)
XLA Modules:
  0.0 63.0 jit_solution(12398493106718187794)
XLA Ops:
  0.0 1.0 %multiply_convert_fusion = bf16[4,32,256]{2,1,0:T(8,128)(2,1)S(1)} fusion(f32[4,32,256]{2,1,0:T(8,128)} %cur.1, f32[4,32,256]{2,1,0:T(8,128)} %noise.1), kind=kLoop, calls=%fused_computation.37 | loop fusion | flops 131072 | bytes 327680 | tf_op jit(solution)/shard_map/convert_element_type | solution.py:403
  1.1 0.7 %convert_element_type.52 = bf16[12,4,32]{2,1,0:T(4,128)(2,1)S(1)} convert(f32[12,4,32]{2,1,0:T(4,128)} %param.12) | non-fusion elementwise | flops 1536 | bytes 9216 | tf_op jit(solution)/shard_map/convert_element_type | solution.py:404
  1.9 0.1 broadcast_in_dim.56
  2.0 0.1 select_select_fusion
  2.1 0.8 %pad_maximum_fusion.1 = bf16[16,84,128]{2,1,0:T(8,128)(2,1)} fusion(bf16[16,12,128]{2,1,0:T(8,128)(2,1)S(1)} %broadcast_in_dim.57, bf16[16,72,128]{2,1,0:T(8,128)(2,1)S(1)} %select_select_fusion), kind=kLoop, calls=%fused_computation.15 | loop fusion | flops 688128 | bytes 688128 | tf_op jit(solution)/shard_map/concatenate | solution.py:334
  2.9 5.5 %all-to-all-start = ((bf16[16,84,128]{2,1,0:T(8,128)(2,1)}), bf16[16,84,128]{2,1,0:T(8,128)(2,1)S(1)}, u32[]{:S(2)}, u32[]{:S(2)}) async-start(bf16[16,84,128]{2,1,0:T(8,128)(2,1)} %pad_maximum_fusion.1), calls=%async_computation | async-start | bytes 720896 | tf_op jit(solution)/shard_map/all_to_all | solution.py:335
  8.4 0.7 %fusion.38 = (s32[1]{0:T(128)}, s32[1]{0:T(128)}, s32[1]{0:T(128)}) fusion(s32[16]{0:T(128)S(1)} %copy-done.3, s32[]{:T(128)S(6)} %max.3, s32[]{:T(128)S(6)} %select_n.106, s32[]{:T(128)S(6)} %select_n.112), kind=kLoop, calls=%fused_computation.89 | loop fusion | bytes 36 | tf_op jit(solution)/shard_map/dynamic_slice | solution.py:343
  13.1 0.6 copy-done.1
  15.9 1.6 %all-to-all-done = bf16[16,84,128]{2,1,0:T(8,128)(2,1)S(1)} async-done(((bf16[16,84,128]{2,1,0:T(8,128)(2,1)}), bf16[16,84,128]{2,1,0:T(8,128)(2,1)S(1)}, u32[]{:S(2)}, u32[]{:S(2)}) %all-to-all-start) | async-done | bytes 344096 | tf_op jit(solution)/shard_map/all_to_all | solution.py:335
  17.5 0.1 reshape_squeeze.15
  17.7 0.1 collective-permute-start
  18.0 7.4 %collective-permute-done = bf16[78,128]{1,0:T(8,128)(2,1)S(1)} collective-permute-done((bf16[78,128]{1,0:T(8,128)(2,1)S(1)}, bf16[78,128]{1,0:T(8,128)(2,1)S(1)}, u32[]{:S(2)}, u32[]{:S(2)}) %collective-permute-start) | collective-permute-done | bytes 20000 | tf_op jit(solution)/shard_map/ppermute | solution.py:318
  25.5 0.1 rev.9
  25.7 0.1 fusion.35
  25.8 0.1 reshape.88
  25.9 0.1 reshape.92
  26.3 0.1 reshape.93
  26.4 0.1 reshape.90
  26.6 2.8 %collective-permute-start.1 = (bf16[27,128]{1,0:T(8,128)(2,1)S(1)}, bf16[27,128]{1,0:T(8,128)(2,1)S(1)}, u32[]{:S(2)}, u32[]{:S(2)}) collective-permute-start(bf16[27,128]{1,0:T(8,128)(2,1)S(1)} %get-tuple-element.24), channel_id=1, source_target_pairs={{0,1},{1,0},{2,3},{3,2},{4,5},{5,4},{6,7},{7,6},{8,9},{9,8},{10,11... | collective-permute-start | bytes 20744 | tf_op jit(solution)/shard_map/ppermute | solution.py:318
  29.4 0.3 collective-permute-start.2
  29.8 0.6 %add_convert_fusion.flags = s32[2]{0:T(128)} fusion(pred[1]{0:T(512)(128)(4,1)} %bitcast.1, pred[1]{0:T(512)(128)(4,1)} %bitcast), kind=kLoop, calls=%fused_computation.76 | loop fusion | flops 4 | bytes 10 | tf_op jit(solution)/shard_map/stack | solution.py:405
  30.5 0.9 %copy.37.w_out_src = bf16[128,1280]{1,0:T(8,128)(2,1)} copy(bf16[128,1280]{0,1:T(8,128)(2,1)S(1)} %bitcast.51) | data formatting | bytes 655360 | tf_op jit(solution)/shard_map/reshape | solution.py:314
  31.4 0.5 collective-permute-done.1
  31.8 4.8 %collective-permute-done.2 = bf16[27,128]{1,0:T(8,128)(2,1)S(1)} collective-permute-done((bf16[27,128]{1,0:T(8,128)(2,1)S(1)}, bf16[27,128]{1,0:T(8,128)(2,1)S(1)}, u32[]{:S(2)}, u32[]{:S(2)}) %collective-permute-start.2) | collective-permute-done | bytes 6944 | tf_op jit(solution)/shard_map/ppermute | solution.py:318
  36.7 0.1 reshape.95
  36.8 0.1 reshape.96
  36.9 0.2 fusion.25
  37.2 0.2 slice.98
  37.3 0.2 slice.101
  37.5 0.1 fusion.29
  37.8 1.1 %pad_maximum_fusion = bf16[50,16,384]{2,1,0:T(8,128)(2,1)} fusion(bf16[50,12,384]{2,1,0:T(8,128)(2,1)S(1)} %slice.122, bf16[50,4,384]{2,1,0:T(4,128)(2,1)S(1)} %copy.29), kind=kLoop, calls=%fused_computation | loop fusion | flops 1228800 | bytes 1228800 | tf_op jit(solution)/shard_map/concatenate | solution.py:386
  38.9 24.0 %net.1 = f32[4,32,256]{2,1,0:T(8,128)} custom-call(s32[2]{0:T(128)} %add_convert_fusion.flags, bf16[800,384]{1,0:T(8,128)(2,1)} %bitcast.50, f32[4,32,256]{2,1,0:T(8,128)} %cur.1, f32[4,32,256]{2,1,0:T(8,128)} %noise.1, bf16[6,384,256]{2,1,0:T(8,128)(2,1)} %copy-done, bf16[1152,128]{1,0:T(8,128)(2,1)} %bitcast.60, bf16[1152,128]{1,0:T(8,128)(2,1)} %bitcast.61, ...), custom_call_target="tpu_custom_call" | custom-call | tf_op jit(solution)/shard_map/net/pallas_call | solution.py:266
  (69 shorter events, 1.6 us)
Async XLA Ops:
  0.0 8.4 %copy-start.3 = (s32[16]{0:T(128)S(1)}, s32[16]{0:T(128)}, u32[]{:S(2)}) copy-start(s32[16]{0:T(128)} %param.13) | copy-start | bytes 196
  1.0 11.8 %copy-start.2 = (bf16[3,3,16,128]{3,2,1,0:T(8,128)(2,1)S(1)}, bf16[3,3,16,128]{3,2,1,0:T(8,128)(2,1)}, u32[]{:S(2)}) copy-start(bf16[3,3,16,128]{3,2,1,0:T(8,128)(2,1)} %param.14) | copy-start | bytes 110596
  2.9 14.6 %all-to-all-start = ((bf16[16,84,128]{2,1,0:T(8,128)(2,1)}), bf16[16,84,128]{2,1,0:T(8,128)(2,1)S(1)}, u32[]{:S(2)}, u32[]{:S(2)}) async-start(bf16[16,84,128]{2,1,0:T(8,128)(2,1)} %pad_maximum_fusion.1), calls=%async_computation | async-start | bytes 720896 | tf_op jit(solution)/shard_map/all_to_all | solution.py:335
  13.0 0.7 %copy-start.1 = (bf16[3,3,128,4]{2,3,1,0:T(4,128)(2,1)S(1)}, bf16[3,3,128,4]{2,3,1,0:T(4,128)(2,1)}, u32[]{:S(2)}) copy-start(bf16[3,3,128,4]{2,3,1,0:T(4,128)(2,1)} %param.19) | copy-start | bytes 27652
  15.8 14.6 %copy-start = (bf16[6,384,256]{2,1,0:T(8,128)(2,1)}, bf16[6,384,256]{2,1,0:T(8,128)(2,1)S(1)}, u32[]{:S(2)}) copy-start(bf16[6,384,256]{2,1,0:T(8,128)(2,1)S(1)} %constant_dynamic-update-slice_fusion.w_in_src) | copy-start | bytes 3538948
  17.7 7.8 %collective-permute-start = (bf16[78,128]{1,0:T(8,128)(2,1)S(1)}, bf16[78,128]{1,0:T(8,128)(2,1)S(1)}, u32[]{:S(2)}, u32[]{:S(2)}) collective-permute-start(bf16[78,128]{1,0:T(8,128)(2,1)S(1)} %pad_maximum_fusion.4), channel_id=1, source_target_pairs={{0,8},{1,9},{2,10},{3,11},{4,12},{5,13},{6,14},{7,15},{8,0},{9,1},... | collective-permute-start | bytes 59912 | tf_op jit(solution)/shard_map/ppermute | solution.py:318
  26.6 5.2 %collective-permute-start.1 = (bf16[27,128]{1,0:T(8,128)(2,1)S(1)}, bf16[27,128]{1,0:T(8,128)(2,1)S(1)}, u32[]{:S(2)}, u32[]{:S(2)}) collective-permute-start(bf16[27,128]{1,0:T(8,128)(2,1)S(1)} %get-tuple-element.24), channel_id=1, source_target_pairs={{0,1},{1,0},{2,3},{3,2},{4,5},{5,4},{6,7},{7,6},{8,9},{9,8},{10,11... | collective-permute-start | bytes 20744 | tf_op jit(solution)/shard_map/ppermute | solution.py:318
  29.4 7.3 %collective-permute-start.2 = (bf16[27,128]{1,0:T(8,128)(2,1)S(1)}, bf16[27,128]{1,0:T(8,128)(2,1)S(1)}, u32[]{:S(2)}, u32[]{:S(2)}) collective-permute-start(bf16[27,128]{1,0:T(8,128)(2,1)S(1)} %get-tuple-element.25), channel_id=1, source_target_pairs={{0,15},{1,2},{2,1},{3,4},{4,3},{5,6},{6,5},{7,8},{8,7},{9,10},{10,... | collective-permute-start | bytes 20744 | tf_op jit(solution)/shard_map/ppermute | solution.py:318

commit v2 on v1

--- a/solution.py
+++ b/solution.py
@@ -22,7 +22,7 @@
 LEN = EXT_COLS // SEGS
 CLEN = LEN // 2
 GROUPS = 8
-NF, NF2, NC = 4, 4, 5
+NF, NF2, NC = 6, 6, 5
 N1, N2, N3 = 24 // NF, 22 // NF2, 10 // NC
 
 sigma_now = 1.0
@@ -75,6 +75,51 @@
     )
     acc = jnp.dot(lhs, rhs, preferred_element_type=F32).reshape(len(firsts), n, SEGS, 2 * CH)
     return [(acc[i, :, :, :CH], acc[i, :, :, CH:]) for i in range(len(firsts))]
+
+
+def fine_pairs(src, firsts, w):
+    n = LEN
+    zero = jnp.zeros((CH, CH), BF)
+
+    def tap(a, b):
+        return w[(3 * a + b) * CH : (3 * a + b + 1) * CH, :]
+
+    lhs = jnp.concatenate(
+        [
+            jnp.concatenate(
+                [
+                    src[base + step * k, b : b + n].reshape(n * SEGS, CH)
+                    for k in (1, 2)
+                    for b in range(3)
+                ],
+                axis=1,
+            )
+            for base, step in firsts
+        ],
+        axis=0,
+    )
+    rhs = jnp.concatenate([w[3 * CH :, :], w[: 6 * CH, :]], axis=0)
+    rhs = jnp.concatenate([rhs[: 6 * CH], rhs[6 * CH :]], axis=1)
+    inner = jnp.dot(lhs, rhs, preferred_element_type=F32).reshape(len(firsts), n, SEGS, 2 * CH)
+    outer = []
+    for k, a in ((0, 0), (3, 2)):
+        parts = []
+        for base, step in firsts:
+            row = src[base + step * k].reshape(CLEN + 1, 2, SEGS, CH)
+            cols = [row[i : i + CLEN, j].reshape(CLEN * SEGS, CH) for i in range(2) for j in range(2)]
+            parts.append(jnp.concatenate(cols, axis=1))
+        even = jnp.concatenate([tap(a, 0), tap(a, 1), tap(a, 2), zero], axis=0)
+        odd = jnp.concatenate([zero, tap(a, 0), tap(a, 1), tap(a, 2)], axis=0)
+        got = jnp.dot(
+            jnp.concatenate(parts, axis=0),
+            jnp.concatenate([even, odd], axis=1),
+            preferred_element_type=F32,
+        ).reshape(len(firsts), CLEN, SEGS, 2 * CH)
+        outer.append(jnp.stack([got[..., :CH], got[..., CH:]], axis=2).reshape(len(firsts), n, SEGS, CH))
+    return [
+        (inner[i, :, :, :CH] + outer[0][i], inner[i, :, :, CH:] + outer[1][i])
+        for i in range(len(firsts))
+    ]
 
 
 def net_kernel(
@@ -167,7 +212,7 @@
 
     def first_body(p, carry):
         firsts = [pair_rows(2 * NF * p + 2 * i - 8, ROWS, top, bottom) for i in range(NF)]
-        outs = conv_pairs(act, [(base + 9, step) for base, step in firsts], w_f1, LEN)
+        outs = fine_pairs(act, [(base + 9, step) for base, step in firsts], w_f1)
         for (base, step), (o0, o1) in zip(firsts, outs):
             put_row(hid, base + step + 8, silu(o0), LEN)
             put_row(hid, base + 2 * step + 8, silu(o1), LEN)
@@ -178,7 +223,7 @@
 
     def second_pairs(first, count):
         firsts = [pair_rows(2 * (first + i) - 6, ROWS, top, bottom) for i in range(count)]
-        outs = conv_pairs(hid, [(base + 8, step) for base, step in firsts], w_f2, LEN)
+        outs = fine_pairs(hid, [(base + 8, step) for base, step in firsts], w_f2)
         for i, ((base, step), (o0, o1)) in enumerate(zip(firsts, outs)):
             r0 = base + step
             r1 = base + 2 * step

time: 63.5 us -> 62.2 us (0.980)
  Pallas kernels: 24 us -> 22.7 us
    pallas_call x1, Pallas kernels: 24 us -> 22.7 us  [run_net(): pl.pallas_call(net_kernel, out_shape=jax.ShapeDtypeStruct((4, ROWS, COLS)...]
where the time goes in v2:
time: 62.2 us; the launch traced here: 61.7 us
  Pallas kernels  22.7 us (36%)
  waiting for transfers between devices  14.3 us (23%)
  starting transfers between devices  8.75 us (14%)
  between operations  6.29 us (10%)
  other arithmetic  4.88 us (8%)
  local copies, waits for them, and re-layouts  4.84 us (8%)
    pallas_call x1, Pallas kernels, run_net(): pl.pallas_call(net_kernel, out_shape=jax.ShapeDtypeStruct((4, ROWS, COLS)...  22.7 us
    ppermute x3, waiting for transfers between devices, swap(): return lax.ppermute(block, ('lat', 'lon'), pairs)  12.7 us
    all_to_all x1, starting transfers between devices, exchange(): got = lax.all_to_all(sent, 'lat', 0, 0, tiled=True)  5.5 us
    ppermute x3, starting transfers between devices, swap(): return lax.ppermute(block, ('lat', 'lon'), pairs)  3.25 us
    all_to_all x1, waiting for transfers between devices, exchange(): got = lax.all_to_all(sent, 'lat', 0, 0, tiled=True)  1.57 us
  transfers between devices with their start and end apart: 4, of which 4 were waited for; matrix products, arithmetic and copies ran while one was open for 5% of the time, Pallas kernels for 0%

profile of v2, /device:TPU:128, one launch (start us, length us, event | category | flops | bytes accessed | tf_op | source)
XLA Modules:
  0.0 61.7 jit_solution(4285163569747275578)
XLA Ops:
  0.0 1.0 %multiply_convert_fusion = bf16[4,32,256]{2,1,0:T(8,128)(2,1)S(1)} fusion(f32[4,32,256]{2,1,0:T(8,128)} %cur.1, f32[4,32,256]{2,1,0:T(8,128)} %noise.1), kind=kLoop, calls=%fused_computation.37 | loop fusion | flops 131072 | bytes 327680 | tf_op jit(solution)/shard_map/convert_element_type | solution.py:448
  1.1 0.7 %convert_element_type.52 = bf16[12,4,32]{2,1,0:T(4,128)(2,1)S(1)} convert(f32[12,4,32]{2,1,0:T(4,128)} %param.12) | non-fusion elementwise | flops 1536 | bytes 9216 | tf_op jit(solution)/shard_map/convert_element_type | solution.py:449
  1.9 0.1 broadcast_in_dim.56
  2.0 0.1 select_select_fusion
  2.1 0.8 %pad_maximum_fusion.1 = bf16[16,84,128]{2,1,0:T(8,128)(2,1)} fusion(bf16[16,12,128]{2,1,0:T(8,128)(2,1)S(1)} %broadcast_in_dim.57, bf16[16,72,128]{2,1,0:T(8,128)(2,1)S(1)} %select_select_fusion), kind=kLoop, calls=%fused_computation.15 | loop fusion | flops 688128 | bytes 688128 | tf_op jit(solution)/shard_map/concatenate | solution.py:379
  2.9 5.5 %all-to-all-start = ((bf16[16,84,128]{2,1,0:T(8,128)(2,1)}), bf16[16,84,128]{2,1,0:T(8,128)(2,1)S(1)}, u32[]{:S(2)}, u32[]{:S(2)}) async-start(bf16[16,84,128]{2,1,0:T(8,128)(2,1)} %pad_maximum_fusion.1), calls=%async_computation | async-start | bytes 720896 | tf_op jit(solution)/shard_map/all_to_all | solution.py:380
  8.4 0.7 %fusion.38 = (s32[1]{0:T(128)}, s32[1]{0:T(128)}, s32[1]{0:T(128)}) fusion(s32[16]{0:T(128)S(1)} %copy-done.3, s32[]{:T(128)S(6)} %max.3, s32[]{:T(128)S(6)} %select_n.106, s32[]{:T(128)S(6)} %select_n.112), kind=kLoop, calls=%fused_computation.89 | loop fusion | bytes 36 | tf_op jit(solution)/shard_map/dynamic_slice | solution.py:388
  13.1 0.6 copy-done.1
  15.9 1.6 %all-to-all-done = bf16[16,84,128]{2,1,0:T(8,128)(2,1)S(1)} async-done(((bf16[16,84,128]{2,1,0:T(8,128)(2,1)}), bf16[16,84,128]{2,1,0:T(8,128)(2,1)S(1)}, u32[]{:S(2)}, u32[]{:S(2)}) %all-to-all-start) | async-done | bytes 344096 | tf_op jit(solution)/shard_map/all_to_all | solution.py:380
  17.5 0.1 reshape_squeeze.15
  17.7 0.1 collective-permute-start
  18.0 7.4 %collective-permute-done = bf16[78,128]{1,0:T(8,128)(2,1)S(1)} collective-permute-done((bf16[78,128]{1,0:T(8,128)(2,1)S(1)}, bf16[78,128]{1,0:T(8,128)(2,1)S(1)}, u32[]{:S(2)}, u32[]{:S(2)}) %collective-permute-start) | collective-permute-done | bytes 20000 | tf_op jit(solution)/shard_map/ppermute | solution.py:363
  25.5 0.1 rev.9
  25.7 0.1 fusion.35
  25.8 0.1 reshape.88
  25.9 0.1 reshape.92
  26.3 0.1 reshape.93
  26.4 0.1 reshape.90
  26.6 2.8 %collective-permute-start.1 = (bf16[27,128]{1,0:T(8,128)(2,1)S(1)}, bf16[27,128]{1,0:T(8,128)(2,1)S(1)}, u32[]{:S(2)}, u32[]{:S(2)}) collective-permute-start(bf16[27,128]{1,0:T(8,128)(2,1)S(1)} %get-tuple-element.24), channel_id=1, source_target_pairs={{0,1},{1,0},{2,3},{3,2},{4,5},{5,4},{6,7},{7,6},{8,9},{9,8},{10,11... | collective-permute-start | bytes 20744 | tf_op jit(solution)/shard_map/ppermute | solution.py:363
  29.4 0.3 collective-permute-start.2
  29.8 0.6 %add_convert_fusion.flags = s32[2]{0:T(128)} fusion(pred[1]{0:T(512)(128)(4,1)} %bitcast.1, pred[1]{0:T(512)(128)(4,1)} %bitcast), kind=kLoop, calls=%fused_computation.76 | loop fusion | flops 4 | bytes 10 | tf_op jit(solution)/shard_map/stack | solution.py:450
  30.5 0.9 %copy.37.w_out_src = bf16[128,1280]{1,0:T(8,128)(2,1)} copy(bf16[128,1280]{0,1:T(8,128)(2,1)S(1)} %bitcast.51) | data formatting | bytes 655360 | tf_op jit(solution)/shard_map/reshape | solution.py:359
  31.4 0.5 collective-permute-done.1
  31.8 4.8 %collective-permute-done.2 = bf16[27,128]{1,0:T(8,128)(2,1)S(1)} collective-permute-done((bf16[27,128]{1,0:T(8,128)(2,1)S(1)}, bf16[27,128]{1,0:T(8,128)(2,1)S(1)}, u32[]{:S(2)}, u32[]{:S(2)}) %collective-permute-start.2) | collective-permute-done | bytes 6944 | tf_op jit(solution)/shard_map/ppermute | solution.py:363
  36.7 0.1 reshape.95
  36.8 0.1 reshape.96
  36.9 0.2 fusion.25
  37.2 0.2 slice.98
  37.3 0.2 slice.101
  37.5 0.1 fusion.29
  37.8 1.1 %pad_maximum_fusion = bf16[50,16,384]{2,1,0:T(8,128)(2,1)} fusion(bf16[50,12,384]{2,1,0:T(8,128)(2,1)S(1)} %slice.122, bf16[50,4,384]{2,1,0:T(4,128)(2,1)S(1)} %copy.29), kind=kLoop, calls=%fused_computation | loop fusion | flops 1228800 | bytes 1228800 | tf_op jit(solution)/shard_map/concatenate | solution.py:431
  38.9 22.7 %net.1 = f32[4,32,256]{2,1,0:T(8,128)} custom-call(s32[2]{0:T(128)} %add_convert_fusion.flags, bf16[800,384]{1,0:T(8,128)(2,1)} %bitcast.50, f32[4,32,256]{2,1,0:T(8,128)} %cur.1, f32[4,32,256]{2,1,0:T(8,128)} %noise.1, bf16[6,384,256]{2,1,0:T(8,128)(2,1)} %copy-done, bf16[1152,128]{1,0:T(8,128)(2,1)} %bitcast.60, bf16[1152,128]{1,0:T(8,128)(2,1)} %bitcast.61, ...), custom_call_target="tpu_custom_call" | custom-call | tf_op jit(solution)/shard_map/net/pallas_call | solution.py:311
  (69 shorter events, 1.6 us)
Async XLA Ops:
  0.0 8.4 %copy-start.3 = (s32[16]{0:T(128)S(1)}, s32[16]{0:T(128)}, u32[]{:S(2)}) copy-start(s32[16]{0:T(128)} %param.13) | copy-start | bytes 196
  1.0 11.8 %copy-start.2 = (bf16[3,3,16,128]{3,2,1,0:T(8,128)(2,1)S(1)}, bf16[3,3,16,128]{3,2,1,0:T(8,128)(2,1)}, u32[]{:S(2)}) copy-start(bf16[3,3,16,128]{3,2,1,0:T(8,128)(2,1)} %param.14) | copy-start | bytes 110596
  2.9 14.6 %all-to-all-start = ((bf16[16,84,128]{2,1,0:T(8,128)(2,1)}), bf16[16,84,128]{2,1,0:T(8,128)(2,1)S(1)}, u32[]{:S(2)}, u32[]{:S(2)}) async-start(bf16[16,84,128]{2,1,0:T(8,128)(2,1)} %pad_maximum_fusion.1), calls=%async_computation | async-start | bytes 720896 | tf_op jit(solution)/shard_map/all_to_all | solution.py:380
  13.0 0.7 %copy-start.1 = (bf16[3,3,128,4]{2,3,1,0:T(4,128)(2,1)S(1)}, bf16[3,3,128,4]{2,3,1,0:T(4,128)(2,1)}, u32[]{:S(2)}) copy-start(bf16[3,3,128,4]{2,3,1,0:T(4,128)(2,1)} %param.19) | copy-start | bytes 27652
  15.8 14.6 %copy-start = (bf16[6,384,256]{2,1,0:T(8,128)(2,1)}, bf16[6,384,256]{2,1,0:T(8,128)(2,1)S(1)}, u32[]{:S(2)}) copy-start(bf16[6,384,256]{2,1,0:T(8,128)(2,1)S(1)} %constant_dynamic-update-slice_fusion.w_in_src) | copy-start | bytes 3538948
  17.7 7.8 %collective-permute-start = (bf16[78,128]{1,0:T(8,128)(2,1)S(1)}, bf16[78,128]{1,0:T(8,128)(2,1)S(1)}, u32[]{:S(2)}, u32[]{:S(2)}) collective-permute-start(bf16[78,128]{1,0:T(8,128)(2,1)S(1)} %pad_maximum_fusion.4), channel_id=1, source_target_pairs={{0,8},{1,9},{2,10},{3,11},{4,12},{5,13},{6,14},{7,15},{8,0},{9,1},... | collective-permute-start | bytes 59912 | tf_op jit(solution)/shard_map/ppermute | solution.py:363
  26.6 5.2 %collective-permute-start.1 = (bf16[27,128]{1,0:T(8,128)(2,1)S(1)}, bf16[27,128]{1,0:T(8,128)(2,1)S(1)}, u32[]{:S(2)}, u32[]{:S(2)}) collective-permute-start(bf16[27,128]{1,0:T(8,128)(2,1)S(1)} %get-tuple-element.24), channel_id=1, source_target_pairs={{0,1},{1,0},{2,3},{3,2},{4,5},{5,4},{6,7},{7,6},{8,9},{9,8},{10,11... | collective-permute-start | bytes 20744 | tf_op jit(solution)/shard_map/ppermute | solution.py:363
  29.4 7.3 %collective-permute-start.2 = (bf16[27,128]{1,0:T(8,128)(2,1)S(1)}, bf16[27,128]{1,0:T(8,128)(2,1)S(1)}, u32[]{:S(2)}, u32[]{:S(2)}) collective-permute-start(bf16[27,128]{1,0:T(8,128)(2,1)S(1)} %get-tuple-element.25), channel_id=1, source_target_pairs={{0,15},{1,2},{2,1},{3,4},{4,3},{5,6},{6,5},{7,8},{8,7},{9,10},{10,... | collective-permute-start | bytes 20744 | tf_op jit(solution)/shard_map/ppermute | solution.py:363
